TPU v7x, 32 devices: a whole 2x2x4 slice. The times are simulated.
32 devices in a mesh: arc: 8 (over z, core), col: 4 (over y, x).
Axes of the slice: x: 2, y: 2, z: 4, core: 2. Of those that a mesh axis runs over, the one named last changes fastest.
Arguments:
- design: bfloat16 [12288, 5120], P('arc', 'col'), may hold values from -0.109375 to 0.109375
- local_design: float32 [16, 12288], P(None, 'arc'), may hold values from -6 to 6
- observed: float32 [12288], P('arc'), may hold values from -6 to 6
- valid_mask: int32 [12288], P('arc'), may hold values 0 or 1
- counts: int32 [64], P('arc'), may hold values from 1 to 192, 7680 in all
Outputs:
- normal: float32 [5120, 5120], P('arc', 'col')
- rhs: float32 [5120], P('col')
Inputs may be any that keep to these rules, and one draw needn't show every extreme that they name: Arc a holds counts[a] recorded slots at its start; the rest are padding.
All inputs are finite; a program needn't handle non-finite values. No bound on the sum of `valid_mask` or of `counts` on one device may be relied on, other than what follows from the above.
Results may differ from a plain program's by a relative error of at most 0.0028.
Values may be sent and summed in bfloat16 or wider, within the bound.
A program may use at most 128 MiB of HBM per device.

v0:
```python
import jax
import jax.numpy as jnp
from jax import lax
from jax.sharding import PartitionSpec as P


def eliminate(block_design, block_local, block_observed, block_live):
    highest = lax.Precision.HIGHEST
    masked = block_local * block_live[None, :]
    gram_matrix = jnp.dot(masked, block_local.T, precision=highest) + jnp.eye(
        block_local.shape[0], dtype=jnp.float32
    )
    factor = jnp.linalg.cholesky(gram_matrix)
    inverse = jax.scipy.linalg.cho_solve(
        (factor, True), jnp.eye(block_local.shape[0], dtype=jnp.float32)
    )
    dense = block_design.astype(jnp.float32)
    cross_terms = jnp.dot(masked, dense, precision=highest)
    cross_obs = jnp.dot(masked, block_observed, precision=highest)
    projector = jnp.dot(inverse, cross_terms, precision=highest)
    projected = block_live[:, None] * (dense - jnp.dot(block_local.T, projector, precision=highest))
    solved_obs = jnp.dot(inverse, cross_obs, precision=highest)
    residual = block_live * (block_observed - jnp.dot(block_local.T, solved_obs, precision=highest))
    return (projected.astype(jnp.bfloat16), residual)


def column_product(column_piece, projected):
    return lax.dot_general(
        column_piece, projected, (((0,), (0,)), ((), ())), preferred_element_type=jnp.float32
    )


def shards(design, local_design, observed, valid_mask, counts):
    row_count, col_width = design.shape
    arc_count = counts.shape[0]
    slot_count = row_count // arc_count
    local_count = local_design.shape[0]
    inside = jnp.arange(slot_count, dtype=jnp.int32)[None, :] < counts[:, None]
    live_mask = inside.reshape(-1).astype(jnp.float32) * valid_mask.astype(jnp.float32)
    blocks_local = local_design.reshape(local_count, arc_count, slot_count).transpose(1, 0, 2)
    projected, residual = jax.vmap(eliminate)(
        design.reshape(arc_count, slot_count, col_width),
        blocks_local,
        observed.reshape(arc_count, slot_count),
        live_mask.reshape(arc_count, slot_count),
    )
    projected = projected.reshape(row_count, col_width)
    rhs_part = jnp.dot(
        residual.reshape(row_count), projected.astype(jnp.float32), precision=lax.Precision.HIGHEST
    )
    gathered = lax.all_gather(projected, "col", axis=1, tiled=True)
    normal = lax.psum_scatter(
        column_product(gathered, projected), "arc", scatter_dimension=0, tiled=True
    )
    rhs = lax.psum(rhs_part, "arc")
    return (normal, rhs)


def solution(mesh):
    placed = (P("arc", "col"), P(None, "arc"), P("arc"), P("arc"), P("arc"))
    return jax.shard_map(
        shards, mesh=mesh, in_specs=placed, out_specs=(P("arc", "col"), P("col")), check_vma=False
    )
```

profile of v0, /device:TPU:0, one launch (start us, length us, event | category | flops | bytes accessed | tf_op | source)
XLA Modules:
  0.0 489.1 jit_solution(5814584548888950459)
XLA Ops:
  7.2 0.0 all-gather.2.cloned.1.call-start
  7.2 0.7 iota_compare_fusion.3
  8.0 0.1 lt.20
  8.1 0.7 convert_select_fusion
  8.8 0.1 mul.28
  8.8 1.0 reshape.48
  9.8 0.3 fusion.5
  10.1 0.1 copy.12
  10.2 11.7 %custom-call.11 = f32[8,16,16]{2,1,0:T(8,128)S(1)} custom-call(f32[8,16,16]{2,1,0:T(8,128)S(1)} %fusion.24), custom_call_target="Cholesky" | custom-call | tf_op jit(solution)/shard_map/vmap(jit(cholesky))/cholesky | solution.py:13
  22.0 0.1 compare_reduce_fusion
  22.1 0.1 select_bitcast_fusion
  22.2 9.8 %custom-call.12 = f32[8,1,16,16]{2,3,1,0:T(8,128)S(1)} custom-call(f32[8,1,16,16]{3,2,1,0:T(8,128)S(1)} %select_bitcast_fusion), custom_call_target="InvertDiagBlocksLowerTriangular" | custom-call | tf_op jit(solution)/shard_map/vmap(jit(_cho_solve))/triangular_solve | solution.py:14
  32.0 0.4 fusion.21
  32.4 0.2 fusion.19
  32.6 4.0 fusion.8
  36.7 0.7 fusion.34
  37.3 0.0 copy-done
  37.3 8.3 %fusion.1 = bf16[8,192,1280]{2,1,0:T(8,128)(2,1)} fusion(bf16[8,192,1280]{2,1,0:T(8,128)(2,1)S(1)} %bitcast.70, f32[8,16,1280]{2,1,0:T(8,128)S(1)} %fusion.34, f32[8,192]{1,0:T(8,128)S(1)} %mul.28, f32[16,8,192]{2,1,0:T(8,128)S(1)} %reshape.48), kind=kOutput, calls=%fused_computation.2 | convolution fusion | flops 385351680 | bytes 8624128 | tf_op jit(solution)/shard_map/vmap()/dot_general | solution.py:21
  45.6 0.0 all-gather.2.cloned.1.call-update
  45.6 0.2 reduce-scatter.2.cloned.1.call-start
  45.8 151.2 %all-gather.2.cloned.1.call-done = bf16[1536,5120]{1,0:T(8,128)(2,1)} async-done(((bf16[1536,1280]{1,0:T(8,128)(2,1)}), bf16[1536,5120]{1,0:T(8,128)(2,1)}) %all-gather.2.cloned.1.call-update) | async-done | bytes 15728656 | tf_op jit(solution)/shard_map/all_gather | solution.py:51
  197.1 27.5 %fusion.35 = f32[5120,1280]{1,0:T(8,128)} fusion(bf16[1536,5120]{1,0:T(8,128)(2,1)} %all-gather.2.cloned.1.call-done, bf16[1536,1280]{1,0:T(8,128)(2,1)} %bitcast.68), kind=kOutput, calls=%fused_computation.49 | convolution fusion | flops 20132659200 | bytes 45875200 | tf_op jit(solution)/shard_map/dot_general | solution.py:28
  224.5 0.0 reduce-scatter.2.cloned.1.call-update
  224.6 0.7 copy-done.1
  225.2 0.1 reshape.60
  225.3 0.1 reshape.50
  225.4 0.3 convolution_bitcast_fusion.1
  225.7 0.2 convolution_bitcast_fusion
  225.9 0.2 fusion.2
  226.1 3.8 convolution_reduce_fusion
  229.9 18.2 %psum.7 = f32[1280]{0:T(1024)} all-reduce(f32[1280]{0:T(1024)S(1)} %convolution_reduce_fusion), channel_id=1, replica_groups=mesh['arc'=8,'col'=4] {'arc'}, use_global_device_ids=true, to_apply=%region_3.4 | all-reduce | flops 1280 | bytes 10240 | tf_op jit(solution)/shard_map/psum | solution.py:55
  248.2 234.1 %reduce-scatter.2.cloned.1.call-done = f32[640,1280]{1,0:T(8,128)} async-done(((f32[5120,1280]{1,0:T(8,128)}), f32[640,1280]{1,0:T(8,128)}) %reduce-scatter.2.cloned.1.call-update) | async-done | bytes 3276816 | tf_op jit(solution)/shard_map/reduce_scatter | solution.py:52
  (8 shorter events, 0.1 us)
Async XLA Ops:
  7.2 189.9 %all-gather.2.cloned.1.call-start = ((), (), s32[]{:S(2)}) async-start(), calls=%async_computation.1 | async-start | bytes 19660800 | tf_op jit(solution)/shard_map/all_gather | solution.py:51
  32.0 5.3 %copy-start = (bf16[1536,1280]{1,0:T(8,128)(2,1)S(1)}, bf16[1536,1280]{1,0:T(8,128)(2,1)}, u32[]{:S(2)}) copy-start(bf16[1536,1280]{1,0:T(8,128)(2,1)} %param.5) | copy-start | bytes 11796484
  45.6 436.6 %reduce-scatter.2.cloned.1.call-start = ((), (), s32[]{:S(2)}) async-start(), calls=%async_computation.2 | async-start | bytes 29491200 | tf_op jit(solution)/shard_map/reduce_scatter | solution.py:52
  224.5 0.7 copy-start.1
Sparse Core Ops, SparseCore 0:
  45.7 151.2 all-gather.1
  224.7 257.5 reduce-scatter.1
where the time goes:
time: 489 us
  waiting for transfers between devices  385 us (79%)
  matrix products  45.8 us (9%)
  other arithmetic  23.3 us (5%)
  blocking collectives  18.2 us (4%)
  between operations  14.2 us (3%)
    reduce_scatter x1, waiting for transfers between devices, shards(): lax.psum_scatter(column_product(gathered, projected), 'arc', scatter_dime...  234 us
    all_gather x1, waiting for transfers between devices, shards(): gathered = lax.all_gather(projected, 'col', axis=1, tiled=True)  151 us
    dot_general x1, matrix products, column_product(): lax.dot_general(column_piece, projected, (((0,), (0,)), ((), ())), prefer...  27.5 us
    psum x1, blocking collectives, shards(): rhs = lax.psum(rhs_part, 'arc')  18.2 us
    another operation x4, other arithmetic, eliminate(): factor = jnp.linalg.cholesky(gram_matrix)  11.9 us
    another operation x3, other arithmetic, eliminate(): jax.scipy.linalg.cho_solve((factor, True), jnp.eye(block_local.shape[0],...  9.94 us
  transfers between devices with their start and end apart: 2, of which 2 were waited for; matrix products, arithmetic and copies ran while one was open for 1% of the time, Pallas kernels for 0%

commit v1 on v0

--- a/solution.py
+++ b/solution.py
@@ -2,6 +2,11 @@
 import jax.numpy as jnp
 from jax import lax
 from jax.sharding import PartitionSpec as P
+
+
+def windows_write(slab_in, chip_axis):
+    t1 = jnp.concatenate(lax.all_gather(slab_in, chip_axis), axis=1)
+    return t1
 
 
 def eliminate(block_design, block_local, block_observed, block_live):
@@ -48,7 +53,7 @@
     rhs_part = jnp.dot(
         residual.reshape(row_count), projected.astype(jnp.float32), precision=lax.Precision.HIGHEST
     )
-    gathered = lax.all_gather(projected, "col", axis=1, tiled=True)
+    gathered = windows_write(projected, chip_axis="col")
     normal = lax.psum_scatter(
         column_product(gathered, projected), "arc", scatter_dimension=0, tiled=True
     )

time: 489 us -> 510 us (1.043)
  local copies, waits for them, and re-layouts: 2.05 us -> 22.7 us
    all_gather x0 -> x1, local copies, waits for them, and re-layouts: none -> 20.6 us  [windows_write(): t1 = jnp.concatenate(lax.all_gather(slab_in, chip_axis), axis=1)]
where the time goes in v1:
time: 510 us; the launch traced here: 509 us
  waiting for transfers between devices  385 us (75%)
  matrix products  45.4 us (9%)
  other arithmetic  23.3 us (5%)
  local copies, waits for them, and re-layouts  22.7 us (4%)
  blocking collectives  18.2 us (4%)
  between operations  14.2 us (3%)
    reduce_scatter x1, waiting for transfers between devices, shards(): lax.psum_scatter(column_product(gathered, projected), 'arc', scatter_dime...  234 us
    all_gather x1, waiting for transfers between devices, windows_write(): t1 = jnp.concatenate(lax.all_gather(slab_in, chip_axis), axis=1)  151 us
    dot_general x1, matrix products, column_product(): lax.dot_general(column_piece, projected, (((0,), (0,)), ((), ())), prefer...  27.2 us
    all_gather x1, local copies, waits for them, and re-layouts, windows_write(): t1 = jnp.concatenate(lax.all_gather(slab_in, chip_axis), axis=1)  20.6 us
    psum x1, blocking collectives, shards(): rhs = lax.psum(rhs_part, 'arc')  18.2 us
    another operation x4, other arithmetic, eliminate(): factor = jnp.linalg.cholesky(gram_matrix)  11.9 us
  transfers between devices with their start and end apart: 2, of which 2 were waited for; matrix products, arithmetic and copies ran while one was open for 1% of the time, Pallas kernels for 0%

profile of v1, /device:TPU:0, one launch (start us, length us, event | category | flops | bytes accessed | tf_op | source)
XLA Modules:
  0.0 509.4 jit_solution(10087815201870254478)
XLA Ops:
  7.2 0.0 all-gather.2.cloned.1.call-start
  7.2 0.7 iota_compare_fusion.3
  8.0 0.1 lt.20
  8.1 0.7 convert_select_fusion
  8.8 0.1 mul.28
  8.8 1.0 reshape.54
  9.8 0.3 fusion.5
  10.1 0.1 copy.21
  10.2 11.7 %custom-call.11 = f32[8,16,16]{2,1,0:T(8,128)S(1)} custom-call(f32[8,16,16]{2,1,0:T(8,128)S(1)} %fusion.24), custom_call_target="Cholesky" | custom-call | tf_op jit(solution)/shard_map/vmap(jit(cholesky))/cholesky | solution.py:18
  22.0 0.1 compare_reduce_fusion
  22.1 0.1 select_bitcast_fusion
  22.2 9.8 %custom-call.12 = f32[8,1,16,16]{2,3,1,0:T(8,128)S(1)} custom-call(f32[8,1,16,16]{3,2,1,0:T(8,128)S(1)} %select_bitcast_fusion), custom_call_target="InvertDiagBlocksLowerTriangular" | custom-call | tf_op jit(solution)/shard_map/vmap(jit(_cho_solve))/triangular_solve | solution.py:19
  32.0 0.4 fusion.21
  32.4 0.2 fusion.19
  32.6 4.0 fusion.8
  36.6 0.7 fusion.34
  37.3 8.2 %fusion.1 = bf16[8,192,1280]{2,1,0:T(8,128)(2,1)} fusion(bf16[8,192,1280]{2,1,0:T(8,128)(2,1)S(1)} %bitcast.74, f32[8,16,1280]{2,1,0:T(8,128)S(1)} %fusion.34, f32[8,192]{1,0:T(8,128)S(1)} %mul.28, f32[16,8,192]{2,1,0:T(8,128)S(1)} %reshape.54), kind=kOutput, calls=%fused_computation.2 | convolution fusion | flops 385351680 | bytes 8624128 | tf_op jit(solution)/shard_map/vmap()/dot_general | solution.py:26
  45.5 0.0 all-gather.2.cloned.1.call-update
  45.6 0.2 reduce-scatter.2.cloned.1.call-start
  45.8 151.2 %all-gather.2.cloned.1.call-done = bf16[4,1536,1280]{2,1,0:T(8,128)(2,1)} async-done(((bf16[1,1536,1280]{2,1,0:T(8,128)(2,1)}), bf16[4,1536,1280]{2,1,0:T(8,128)(2,1)}) %all-gather.2.cloned.1.call-update) | async-done | bytes 15728656 | tf_op jit(solution)/shard_map/all_gather | solution.py:8
  197.0 20.6 %copy.23 = bf16[4,1536,1280]{1,2,0:T(8,128)(2,1)} copy(bf16[4,1536,1280]{2,1,0:T(8,128)(2,1)} %all-gather.2.cloned.1.call-done) | data formatting | bytes 31457280 | tf_op jit(solution)/shard_map/all_gather | solution.py:8
  217.7 27.2 %fusion.35 = f32[5120,1280]{1,0:T(8,128)} fusion(bf16[1536,5120]{0,1:T(8,128)(2,1)} %bitcast.75, bf16[1536,1280]{1,0:T(8,128)(2,1)} %bitcast.72), kind=kOutput, calls=%fused_computation.49 | convolution fusion | flops 20132659200 | bytes 45875200 | tf_op jit(solution)/shard_map/dot_general | solution.py:33
  244.8 0.0 reduce-scatter.2.cloned.1.call-update
  244.8 0.7 copy-done.1
  245.5 0.1 reshape.68
  245.6 0.1 reshape.58
  245.7 0.3 convolution_bitcast_fusion.1
  245.9 0.2 convolution_bitcast_fusion
  246.2 0.2 fusion.2
  246.4 3.8 convolution_reduce_fusion
  250.2 18.2 %psum.7 = f32[1280]{0:T(1024)} all-reduce(f32[1280]{0:T(1024)S(1)} %convolution_reduce_fusion), channel_id=1, replica_groups=mesh['arc'=8,'col'=4] {'arc'}, use_global_device_ids=true, to_apply=%region_3.4 | all-reduce | flops 1280 | bytes 10240 | tf_op jit(solution)/shard_map/psum | solution.py:60
  268.4 234.1 %reduce-scatter.2.cloned.1.call-done = f32[640,1280]{1,0:T(8,128)} async-done(((f32[5120,1280]{1,0:T(8,128)}), f32[640,1280]{1,0:T(8,128)}) %reduce-scatter.2.cloned.1.call-update) | async-done | bytes 3276816 | tf_op jit(solution)/shard_map/reduce_scatter | solution.py:57
  (9 shorter events, 0.1 us)
Async XLA Ops:
  7.2 189.9 %all-gather.2.cloned.1.call-start = ((), (), s32[]{:S(2)}) async-start(), calls=%async_computation.1 | async-start | bytes 19660800 | tf_op jit(solution)/shard_map/all_gather | solution.py:8
  32.0 5.3 %copy-start = (bf16[1536,1280]{1,0:T(8,128)(2,1)S(1)}, bf16[1536,1280]{1,0:T(8,128)(2,1)}, u32[]{:S(2)}) copy-start(bf16[1536,1280]{1,0:T(8,128)(2,1)} %param.5) | copy-start | bytes 11796484
  45.6 457.0 %reduce-scatter.2.cloned.1.call-start = ((), (), s32[]{:S(2)}) async-start(), calls=%async_computation.2 | async-start | bytes 29491200 | tf_op jit(solution)/shard_map/reduce_scatter | solution.py:57
  244.8 0.7 copy-start.1
Sparse Core Ops, SparseCore 0:
  45.7 151.2 all-gather.1
  245.0 257.5 reduce-scatter.1
